TPU v7x, 32 devices: a whole 2x2x4 slice. The times are simulated.
32 devices in a mesh: band: 4 (over y, core), lev: 8 (over z, x).
Axes of the slice: x: 2, y: 2, z: 4, core: 2. Of those that a mesh axis runs over, the one named last changes fastest.
Arguments:
- azimuthal_coeffs: bfloat16 [2560, 64, 64], P('band', 'lev'), may hold values from -6 to 6
- polynomial_tables: bfloat16 [32, 2, 448, 1280], P(('band', 'lev')), may hold values from -0.15625 to 0.15625
- gauss_masses: float32 [1280], replicated, may hold values from 0.3 to 1.5
- circle_samples: int32 [1280], replicated, may hold values from 20 to 152, as said below
- table_lookup: int32 [32], replicated, may hold values from 0 to 31, each once
- eigen_basis: float32 [16, 16], replicated, may hold values from -1.5 to 1.5
- basis_mapping: float32 [16, 16], replicated, may hold values from -1.5 to 1.5
- eigen_constants: float32 [16], replicated, may hold values from 0.5 to 2
- hydrostatic_matrix: float32 [16, 16], replicated, may hold values from -1.5 to 1.5
- thermal_response: float32 [16, 16], replicated, may hold values from -1.5 to 1.5
Outputs:
- advanced: bfloat16 [2560, 64, 64], P('band', 'lev')
Inputs may be any that keep to these rules, and one draw needn't show every extreme that they name: circle_samples[j] is 20 + 4 * floor(j * 32 / 1280) plus 0, 4 or 8; row 0 holds 20 and row 1279 the largest value. table_lookup is a permutation of 0 .. 31.
All inputs are finite; a program needn't handle non-finite values.
Results may differ from a plain program's by a relative error of at most 0.0041.
The roundings to bfloat16 on the way count: a program that leaves them out, or rounds other values in their place, can miss the bound.
Values may be sent and summed in bfloat16 or wider, within the bound.
No kernel may reach another device: no remote copies, remote signals or barrier semaphores. Data moves between devices by JAX's collectives and lax.ppermute only.
A program may use at most 64 MiB of HBM per device.

v0:
```python
import jax
import jax.numpy as jnp
from jax import lax
from jax.sharding import PartitionSpec as P

TRUNC = 1280
FIELDS = 4


TRUNCATION_LIMIT = lax.Precision.HIGHEST
STIFFNESS = 8.0
DIFFUSION = 4.0


def harmonic_advance(
    harmonic_current,
    total_order,
    eigen_basis,
    basis_mapping,
    eigen_constants,
    hydrostatic_matrix,
    thermal_response,
):
    scaled = total_order * (total_order + 1.0) / (TRUNC * (TRUNC + 1.0))
    implicit_weighting = STIFFNESS * scaled
    rotational_curl = harmonic_current[:, 0]
    dilatation_current = harmonic_current[:, 1]
    thermal_current = harmonic_current[:, 2]
    moisture = harmonic_current[:, 3]
    hyper_viscosity = 1.0 / (1.0 + DIFFUSION * scaled * scaled)
    explicit_righthand = dilatation_current + implicit_weighting[:, None, None] * jnp.einsum(
        "li,eic->elc", hydrostatic_matrix, thermal_current, precision=TRUNCATION_LIMIT
    )
    projected = jnp.einsum(
        "li,eic->elc", basis_mapping, explicit_righthand, precision=TRUNCATION_LIMIT
    )
    projected = projected / (
        1.0 + implicit_weighting[:, None, None] * eigen_constants[None, :, None]
    )
    dilatation_future = jnp.einsum(
        "li,eic->elc", eigen_basis, projected, precision=TRUNCATION_LIMIT
    )
    thermal_future = thermal_current - jnp.einsum(
        "li,eic->elc", thermal_response, dilatation_future, precision=TRUNCATION_LIMIT
    )
    return jnp.stack(
        [
            rotational_curl * hyper_viscosity[:, None, None],
            dilatation_future,
            thermal_future,
            moisture * hyper_viscosity[:, None, None],
        ],
        axis=1,
    )


def analyse_wave(column, zonal_order, operator_array, gauss_masses, circle_samples):
    half_rows = operator_array.shape[2]
    live_mask = (2 * zonal_order < circle_samples).astype(jnp.float32)
    north = column[:half_rows].astype(jnp.float32)
    south = jnp.flip(column[half_rows:], axis=0).astype(jnp.float32)
    weight_col = (gauss_masses * live_mask)[:, None]
    even_part = ((north + south) * weight_col).astype(jnp.bfloat16)
    odd_part = ((north - south) * weight_col).astype(jnp.bfloat16)
    spec_even = jnp.dot(operator_array[0], even_part, preferred_element_type=jnp.float32)
    spec_odd = jnp.dot(operator_array[1], odd_part, preferred_element_type=jnp.float32)
    return jnp.stack([spec_even, spec_odd], axis=0)


def complete_harmonic(
    harmonic_coeffs,
    zonal_order,
    operator_array,
    circle_samples,
    eigen_basis,
    basis_mapping,
    eigen_constants,
    hydrostatic_matrix,
    thermal_response,
):
    pair_rows = harmonic_coeffs.shape[1]
    col_count = harmonic_coeffs.shape[2]
    offsets = jnp.arange(pair_rows, dtype=jnp.int32) * 2 + zonal_order
    keep_even = (offsets < TRUNC).astype(jnp.float32)[:, None]
    keep_odd = (offsets + 1 < TRUNC).astype(jnp.float32)[:, None]
    harmonic_current = jnp.concatenate(
        [harmonic_coeffs[0] * keep_even, harmonic_coeffs[1] * keep_odd], axis=0
    )
    total_order = jnp.concatenate([offsets, offsets + 1]).astype(jnp.float32)
    arranged = harmonic_current.reshape(2 * pair_rows, FIELDS, col_count // (2 * FIELDS), 2)
    refreshed = harmonic_advance(
        arranged,
        total_order,
        eigen_basis,
        basis_mapping,
        eigen_constants,
        hydrostatic_matrix,
        thermal_response,
    )
    refreshed = refreshed.reshape(2 * pair_rows, col_count).astype(jnp.bfloat16)
    contract = (((0,), (0,)), ((), ()))
    even_sum = lax.dot_general(
        operator_array[0], refreshed[:pair_rows], contract, preferred_element_type=jnp.float32
    )
    odd_sum = lax.dot_general(
        operator_array[1], refreshed[pair_rows:], contract, preferred_element_type=jnp.float32
    )
    live_col = (2 * zonal_order < circle_samples).astype(jnp.float32)[:, None]
    north_out = (even_sum + odd_sum) * live_col
    south_out = (even_sum - odd_sum) * live_col
    return jnp.concatenate([north_out, jnp.flip(south_out, axis=0)], axis=0).astype(jnp.bfloat16)


def per_device(
    azimuthal_coeffs,
    polynomial_tables,
    gauss_masses,
    circle_samples,
    table_lookup,
    eigen_basis,
    basis_mapping,
    eigen_constants,
    hydrostatic_matrix,
    thermal_response,
):
    lat_rows, level_cols, last_width = azimuthal_coeffs.shape
    wave_count = last_width // 2
    band_count = lax.axis_size("band")
    lev_count = lax.axis_size("lev")
    device_id = lax.axis_index("band") * lev_count + lax.axis_index("lev")
    serial = jnp.arange(wave_count, dtype=jnp.int32)
    wave_of = jnp.zeros((wave_count,), jnp.int32).at[table_lookup].set(serial)
    own_wave = jnp.sum(jnp.where(table_lookup == device_id, serial, 0))
    operator_array = polynomial_tables[0]
    parts = jnp.arange(2, dtype=jnp.int32)[None, :]
    column_pick = (2 * wave_of[:, None] + parts).reshape(-1)
    ordered = jnp.take(azimuthal_coeffs, column_pick, axis=2)
    ordered = ordered.reshape(lat_rows, level_cols, band_count, lev_count, 2)
    ordered = jnp.transpose(ordered, (0, 2, 3, 1, 4)).reshape(
        lat_rows, band_count, lev_count * level_cols * 2
    )
    level_mixed = lax.all_to_all(ordered, "lev", split_axis=2, concat_axis=2, tiled=True)
    harmonic_coeffs = analyse_wave(
        lax.all_to_all(level_mixed, "band", split_axis=1, concat_axis=0, tiled=True)[:, 0, :],
        own_wave,
        operator_array,
        gauss_masses,
        circle_samples,
    )
    result = complete_harmonic(
        harmonic_coeffs,
        own_wave,
        operator_array,
        circle_samples,
        eigen_basis,
        basis_mapping,
        eigen_constants,
        hydrostatic_matrix,
        thermal_response,
    )
    returned = lax.all_to_all(
        lax.all_to_all(result[:, None, :], "band", split_axis=0, concat_axis=1, tiled=True),
        "lev",
        split_axis=2,
        concat_axis=2,
        tiled=True,
    )
    returned = returned.reshape(lat_rows, band_count, lev_count, level_cols, 2)
    returned = jnp.transpose(returned, (0, 3, 1, 2, 4)).reshape(lat_rows, level_cols, last_width)
    back_pick = (2 * table_lookup[:, None] + parts).reshape(-1)
    return jnp.take(returned, back_pick, axis=2)


def solution(mesh):
    placed = (
        P("band", "lev", None),
        P(("band", "lev"), None, None, None),
        P(),
        P(),
        P(),
        P(),
        P(),
        P(),
        P(),
        P(),
    )
    return jax.shard_map(
        per_device, mesh=mesh, in_specs=placed, out_specs=P("band", "lev", None), check_vma=False
    )
```

profile of v0, /device:TPU:0, one launch (start us, length us, event | category | flops | bytes accessed | tf_op | source)
XLA Modules:
  0.0 95.1 jit_solution(13781600453538992396)
XLA Ops:
  0.0 1.4 %broadcast_multiply_fusion = (s32[32]{0:T(128)S(1)}, s32[32]{0:T(128)S(1)}, s32[]{:T(128)}) fusion(s32[32]{0:T(128)} %param.16, s32[]{:T(128)S(6)} %add.120), kind=kLoop, calls=%fused_computation.77 | loop fusion | flops 223 | bytes 392 | tf_op jit(solution)/shard_map/mul | solution.py:170
  1.4 0.7 scatter_custom_fusion
  2.1 0.1 add.118
  2.3 2.5 %gather_fusion = bf16[64,640,8]{1,0,2:T(8,128)(2,1)S(1)} fusion(bf16[640,8,64]{0,2,1:T(8,128)(2,1)S(1)} %copy-done, s32[1024]{0:T(1024)S(1)} %pad_clamp_fusion.1), kind=kCustom, calls=%fused_computation.clone | custom fusion | bytes 1310976 | tf_op jit(solution)/shard_map/jit(_take)/gather | solution.py:137
  4.9 0.1 select_bitcast_fusion.1
  5.0 0.2 reshape.147
  5.3 1.1 %copy.64 = bf16[640,8,4,8,2]{0,2,4,1,3:T(4,128)(2,1)} copy(bf16[640,8,4,8,2]{0,4,3,2,1:T(2,128)(2,1)S(1)} %reshape.147) | data formatting | bytes 1310720 | tf_op jit(solution)/shard_map/reshape | solution.py:138
  6.4 7.3 %all-to-all-start = ((bf16[640,4,128]{0,1,2:T(4,128)(2,1)}), bf16[640,4,128]{0,1,2:T(4,128)(2,1)S(1)}, u32[]{:S(2)}, u32[]{:S(2)}) async-start(bf16[640,4,128]{0,1,2:T(4,128)(2,1)} %bitcast.2), calls=%async_computation | async-start | bytes 1310720 | tf_op jit(solution)/shard_map/all_to_all | solution.py:142
  14.3 0.6 multiply_add_fusion.1
  14.9 0.1 fusion.33
  15.1 15.9 %all-to-all-done = bf16[640,4,128]{0,1,2:T(4,128)(2,1)S(1)} async-done(((bf16[640,4,128]{0,1,2:T(4,128)(2,1)}), bf16[640,4,128]{0,1,2:T(4,128)(2,1)S(1)}, u32[]{:S(2)}, u32[]{:S(2)}) %all-to-all-start) | async-done | bytes 655392 | tf_op jit(solution)/shard_map/all_to_all | solution.py:142
  30.9 0.9 copy.65
  31.9 3.5 %all-to-all-start.1 = ((bf16[640,4,128]{0,2,1:T(8,128)(2,1)}), bf16[640,4,128]{0,2,1:T(8,128)(2,1)S(1)}, u32[]{:S(2)}, u32[]{:S(2)}) async-start(bf16[640,4,128]{0,2,1:T(8,128)(2,1)} %copy.65), calls=%async_computation.1 | async-start | bytes 1310720 | tf_op jit(solution)/shard_map/all_to_all | solution.py:144
  35.3 0.6 compare_convert_fusion
  36.1 9.4 %all-to-all-done.1 = bf16[640,4,128]{0,2,1:T(8,128)(2,1)S(1)} async-done(((bf16[640,4,128]{0,2,1:T(8,128)(2,1)}), bf16[640,4,128]{0,2,1:T(8,128)(2,1)S(1)}, u32[]{:S(2)}, u32[]{:S(2)}) %all-to-all-start.1) | async-done | bytes 655392 | tf_op jit(solution)/shard_map/all_to_all | solution.py:144
  45.5 0.3 copy.66
  45.9 0.3 rev.8
  46.3 2.0 %fusion = f32[448,128]{1,0:T(8,128)S(1)} fusion(bf16[1,2,448,1280]{3,2,1,0:T(8,128)(2,1)} %param.13, bf16[1280,128]{1,0:T(8,128)(2,1)S(1)} %rev.8, bf16[1280,128]{1,0:T(8,128)(2,1)S(1)} %bitcast.105, f32[1280]{0:T(1024)S(1)} %broadcast_select_fusion, f32[448]{0:T(512)S(1)} %get-tuple-element.26), kind=kOutput, calls=%fused_computation.5 | convolution fusion | flops 147677184 | bytes 2038528 | tf_op jit(solution)/shard_map/dot_general | solution.py:65
  48.3 0.6 fusion.1
  48.9 0.2 copy.67
  49.1 0.3 reshape.149
  49.5 0.1 copy-done.2
  49.6 0.2 fusion.11
  49.8 0.2 fusion.9
  50.1 0.2 convolution_bitcast_fusion.1
  50.4 0.2 fusion.13
  50.7 0.1 fusion.41
  50.8 0.1 copy.73
  50.9 0.1 slice.56
  51.0 1.6 %fusion.2 = f32[128,1280]{1,0:T(8,128)S(1)} fusion(bf16[448,128]{0,1:T(8,128)(2,1)S(1)} %slice.56, bf16[1,2,448,1280]{3,2,1,0:T(8,128)(2,1)} %param.13), kind=kOutput, calls=%fused_computation.7 | convolution fusion | flops 146800640 | bytes 1916928 | tf_op jit(solution)/shard_map/dot_general | solution.py:105
  52.7 0.1 copy.72
  52.8 0.1 slice.54
  52.9 1.6 %fusion.5 = f32[128,1280]{1,0:T(8,128)S(1)} fusion(bf16[448,128]{0,1:T(8,128)(2,1)S(1)} %slice.54, bf16[1,2,448,1280]{3,2,1,0:T(8,128)(2,1)} %param.13), kind=kOutput, calls=%fused_computation.10 | convolution fusion | flops 146800640 | bytes 1916928 | tf_op jit(solution)/shard_map/dot_general | solution.py:102
  54.7 1.0 %rev.9 = bf16[1280,128]{0,1:T(8,128)(2,1)S(1)} reverse(bf16[1280,128]{0,1:T(8,128)(2,1)S(1)} %multiply_bitcast_fusion), dimensions={0} | reverse | bytes 655360 | tf_op jit(solution)/shard_map/jit(_flip)/rev | solution.py:111
  55.8 0.5 broadcast.172
  56.3 1.1 %reduce = bf16[2560,128]{0,1:T(8,128)(2,1)S(1)} reduce(bf16[2560,1,128]{0,2,1:T(8,128)(2,1)S(1)} %pad_maximum_fusion, bf16[]{:T(256)} %broadcast.172), dimensions={1}, to_apply=%copy.74.reduce_sub_computation | reduce | bytes 1310722 | tf_op jit(solution)/shard_map/concatenate | solution.py:111
  57.4 0.3 copy.96
  57.7 0.2 reshape.190
  57.9 12.6 %all_to_all.43 = bf16[4,2,40960]{2,1,0:T(2,128)(2,1)S(1)} all-to-all(bf16[4,2,40960]{2,1,0:T(2,128)(2,1)S(1)} %reshape.190), channel_id=1, replica_groups=mesh['band'=4,'lev'=8] {'band'}, dimensions={0} | all-to-all | bytes 1310720 | tf_op jit(solution)/shard_map/all_to_all | solution.py:162
  70.5 0.6 reshape.191
  71.1 0.1 copy.78
  71.2 1.3 %copy.75 = bf16[640,4,128]{0,1,2:T(4,128)(2,1)} copy(bf16[640,4,128]{2,0,1:T(8,128)(2,1)S(1)} %bitcast.102) | data formatting | bytes 1310720 | tf_op jit(solution)/shard_map/all_to_all | solution.py:162
  72.5 3.6 %all-to-all-start.3 = ((bf16[640,4,128]{0,1,2:T(4,128)(2,1)}), bf16[640,4,128]{0,1,2:T(4,128)(2,1)S(1)}, u32[]{:S(2)}, u32[]{:S(2)}) async-start(bf16[640,4,128]{0,1,2:T(4,128)(2,1)} %copy.75), calls=%async_computation.3 | async-start | bytes 1310720 | tf_op jit(solution)/shard_map/all_to_all | solution.py:161
  76.2 0.1 add.133
  76.4 16.8 %all-to-all-done.3 = bf16[640,4,128]{0,1,2:T(4,128)(2,1)S(1)} async-done(((bf16[640,4,128]{0,1,2:T(4,128)(2,1)}), bf16[640,4,128]{0,1,2:T(4,128)(2,1)S(1)}, u32[]{:S(2)}, u32[]{:S(2)}) %all-to-all-start.3) | async-done | bytes 655392 | tf_op jit(solution)/shard_map/all_to_all | solution.py:161
  93.3 0.7 gather_fusion.1
  94.0 0.2 select_bitcast_fusion
  94.1 0.9 copy.77
  (40 shorter events, 0.8 us)
Async XLA Ops:
  0.0 2.3 %copy-start = (bf16[640,8,64]{0,2,1:T(8,128)(2,1)S(1)}, bf16[640,8,64]{0,2,1:T(8,128)(2,1)}, u32[]{:S(2)}) copy-start(bf16[640,8,64]{0,2,1:T(8,128)(2,1)} %param.12) | copy-start | bytes 1966084
  5.3 9.8 %copy-start.4 = (s32[1280]{0:T(1024)S(1)}, s32[1280]{0:T(1024)}, u32[]{:S(2)}) copy-start(s32[1280]{0:T(1024)} %param.15) | copy-start | bytes 15364
  6.4 24.6 %all-to-all-start = ((bf16[640,4,128]{0,1,2:T(4,128)(2,1)}), bf16[640,4,128]{0,1,2:T(4,128)(2,1)S(1)}, u32[]{:S(2)}, u32[]{:S(2)}) async-start(bf16[640,4,128]{0,1,2:T(4,128)(2,1)} %bitcast.2), calls=%async_computation | async-start | bytes 1310720 | tf_op jit(solution)/shard_map/all_to_all | solution.py:142
  15.0 21.0 %copy-start.5 = (f32[1280]{0:T(1024)S(1)}, f32[1280]{0:T(1024)}, u32[]{:S(2)}) copy-start(f32[1280]{0:T(1024)} %param.14) | copy-start | bytes 15364
  15.0 21.0 %copy-start.7 = (f32[16]{0:T(128)S(1)}, f32[16]{0:T(128)}, u32[]{:S(2)}) copy-start(f32[16]{0:T(128)} %param.19) | copy-start | bytes 196
  31.9 13.7 %all-to-all-start.1 = ((bf16[640,4,128]{0,2,1:T(8,128)(2,1)}), bf16[640,4,128]{0,2,1:T(8,128)(2,1)S(1)}, u32[]{:S(2)}, u32[]{:S(2)}) async-start(bf16[640,4,128]{0,2,1:T(8,128)(2,1)} %copy.65), calls=%async_computation.1 | async-start | bytes 1310720 | tf_op jit(solution)/shard_map/all_to_all | solution.py:144
  46.3 2.0 %copy-start.1 = (bf16[1,2,448,1280]{3,2,1,0:T(8,128)(2,1)S(1)}, bf16[1,2,448,1280]{3,2,1,0:T(8,128)(2,1)}, u32[]{:S(2)}) copy-start(bf16[1,2,448,1280]{3,2,1,0:T(8,128)(2,1)} %param.13) | copy-start | bytes 6881284
  48.9 0.7 copy-start.2
  49.1 0.7 copy-start.8
  49.1 1.0 %copy-start.6 = (f32[16,16]{1,0:T(8,128)S(1)}, f32[16,16]{1,0:T(8,128)}, u32[]{:S(2)}) copy-start(f32[16,16]{1,0:T(8,128)} %param.17) | copy-start | bytes 3076
  49.1 1.2 %copy-start.3 = (f32[16,16]{1,0:T(8,128)S(1)}, f32[16,16]{1,0:T(8,128)}, u32[]{:S(2)}) copy-start(f32[16,16]{1,0:T(8,128)} %param.21) | copy-start | bytes 3076
  72.5 20.7 %all-to-all-start.3 = ((bf16[640,4,128]{0,1,2:T(4,128)(2,1)}), bf16[640,4,128]{0,1,2:T(4,128)(2,1)S(1)}, u32[]{:S(2)}, u32[]{:S(2)}) async-start(bf16[640,4,128]{0,1,2:T(4,128)(2,1)} %copy.75), calls=%async_computation.3 | async-start | bytes 1310720 | tf_op jit(solution)/shard_map/all_to_all | solution.py:161
where the time goes:
time: 95.6 us; the launch traced here: 95.1 us
  waiting for transfers between devices  42.2 us (44%)
  starting transfers between devices  14.4 us (15%)
  local copies, waits for them, and re-layouts  13.4 us (14%)
  blocking collectives  12.6 us (13%)
  matrix products  6.71 us (7%)
  other arithmetic  4.69 us (5%)
  between operations  1.12 us (1%)
    all_to_all x1, waiting for transfers between devices, per_device(): lax.all_to_all(lax.all_to_all(result[:, None, :], 'band', split_axis=0, c...  16.8 us
    all_to_all x1, waiting for transfers between devices, per_device(): lax.all_to_all(ordered, 'lev', split_axis=2, concat_axis=2, tiled=True)  15.9 us
    all_to_all x1, blocking collectives, per_device(): lax.all_to_all(result[:, None, :], 'band', split_axis=0, concat_axis=1, t...  12.6 us
    all_to_all x1, waiting for transfers between devices, per_device(): lax.all_to_all(level_mixed, 'band', split_axis=1, concat_axis=0, tiled=True)  9.43 us
    all_to_all x1, starting transfers between devices, per_device(): lax.all_to_all(ordered, 'lev', split_axis=2, concat_axis=2, tiled=True)  7.28 us
    all_to_all x1, starting transfers between devices, per_device(): lax.all_to_all(lax.all_to_all(result[:, None, :], 'band', split_axis=0, c...  3.63 us
    all_to_all x1, starting transfers between devices, per_device(): lax.all_to_all(level_mixed, 'band', split_axis=1, concat_axis=0, tiled=True)  3.48 us
    gather x1, local copies, waits for them, and re-layouts, per_device(): ordered = jnp.take(azimuthal_coeffs, column_pick, axis=2)  2.54 us
  transfers between devices with their start and end apart: 3, of which 3 were waited for; matrix products, arithmetic and copies ran while one was open for 2% of the time, Pallas kernels for 0%

commit v1 on v0

v1 whole, which is shorter than its diff:
```python
import functools

import jax
import jax.numpy as jnp
from jax import lax
from jax.experimental import pallas as pl
from jax.experimental.pallas import tpu as pltpu
from jax.sharding import PartitionSpec as P

TRUNC = 1280
FIELDS = 4
STIFFNESS = 8.0
DIFFUSION = 4.0
LANES = 128
HIGHEST = lax.Precision.HIGHEST
F32 = jnp.float32
BF16 = jnp.bfloat16
I32 = jnp.int32
VMEM_BYTES = 24 * 2**20


def iota(shape, dim):
    return lax.broadcasted_iota(I32, shape, dim)


def dot32(a, b):
    return jnp.dot(a, b, precision=HIGHEST, preferred_element_type=F32)


def owner_rows(lookup, width, columns):
    waves = lookup.shape[1]
    row = iota((1, columns), 1)
    level, place = lax.div(row, width), lax.rem(row, width)
    pick = (iota((waves, columns), 0) == lax.div(lax.rem(iota((waves, columns), 1), width), 2)).astype(F32)
    owner = dot32(lookup.astype(F32), pick).astype(I32)
    per_owner = 2 * (columns // width)
    return owner * per_owner + level * 2 + lax.rem(place, 2)


def send_kernel(width, block, lookup_ref, x_ref, out_ref):
    columns = x_ref.shape[0]
    target = owner_rows(lookup_ref[...], width, columns)
    row = iota((block, columns), 0) + pl.program_id(0) * block
    pick = (row == target).astype(F32).astype(BF16)
    out_ref[...] = jnp.dot(pick, x_ref[...], preferred_element_type=F32).astype(BF16)


def back_kernel(width, block, lookup_ref, x_ref, out_ref):
    columns = x_ref.shape[0]
    waves = lookup_ref.shape[1]
    row = iota((block, 1), 0) + pl.program_id(0) * block
    level, place = lax.div(row, width), lax.rem(row, width)
    mine = iota((block, waves), 1) == lax.div(lax.rem(iota((block, waves), 0) + pl.program_id(0) * block, width), 2)
    owner = jnp.sum(jnp.where(mine, lookup_ref[...].astype(F32), 0.0), axis=1, keepdims=True).astype(I32)
    target = owner * (2 * (columns // width)) + level * 2 + lax.rem(place, 2)
    pick = (iota((block, columns), 1) == target).astype(F32).astype(BF16)
    out_ref[...] = jnp.dot(pick, x_ref[...], preferred_element_type=F32).astype(BF16)


def pair_up(small):
    n = small.shape[0]
    left = (lax.div(iota((2 * n, n), 0), 2) == iota((2 * n, n), 1)).astype(F32)
    right = (iota((n, 2 * n), 0) == lax.div(iota((n, 2 * n), 1), 2)).astype(F32)
    same = lax.rem(iota((2 * n, 2 * n), 0), 2) == lax.rem(iota((2 * n, 2 * n), 1), 2)
    return jnp.where(same, dot32(dot32(left, small), right), 0.0)


def prep_kernel(
    lev_count,
    lookup_ref,
    masses_ref,
    samples_ref,
    eigen_basis_ref,
    basis_mapping_ref,
    eigen_constants_ref,
    hydrostatic_ref,
    thermal_ref,
    rows_ref,
    first_ref,
    second_ref,
    degree_ref,
    scale_ref,
):
    waves = lookup_ref.shape[1]
    me = lax.axis_index("band") * lev_count + lax.axis_index("lev")
    wave = jnp.sum(
        jnp.where(lookup_ref[...] == me, iota((1, waves), 1), 0).astype(F32), axis=1, keepdims=True
    ).astype(I32)
    live = (2 * wave < samples_ref[...]).astype(F32)
    rows_ref[0:1, :] = live
    rows_ref[1:2, :] = masses_ref[...] * live
    n = 2 * eigen_basis_ref.shape[0]
    mapping = pair_up(basis_mapping_ref[...])
    basis = pair_up(eigen_basis_ref[...])
    first_ref[...] = jnp.zeros(first_ref.shape, F32)
    first_ref[0:n, 0:n] = mapping
    first_ref[n : 2 * n, n : 2 * n] = dot32(mapping, pair_up(hydrostatic_ref[...]))
    second_ref[0:n, :] = basis
    second_ref[n : 2 * n, :] = dot32(pair_up(thermal_ref[...]), basis)
    half = n // 2
    spread = lax.div(iota((n, half), 0), 2) == iota((n, half), 1)
    constants = jnp.sum(jnp.where(spread, eigen_constants_ref[...], 0.0), axis=1, keepdims=True)
    nth = degree_ref.shape[2]
    for parity in range(2):
        degree = iota((1, nth), 1) * 2 + wave + parity
        keep = (degree < TRUNC).astype(F32)
        order = degree.astype(F32)
        scaled = order * (order + 1.0) / (TRUNC * (TRUNC + 1.0))
        weight = STIFFNESS * scaled
        degree_ref[parity, 0:1, :] = keep
        degree_ref[parity, 1:2, :] = weight
        degree_ref[parity, 2:3, :] = keep / (1.0 + DIFFUSION * scaled * scaled)
        scale_ref[parity] = 1.0 + weight * constants


def step_kernel(z_ref, table_ref, rows_ref, first_ref, second_ref, degree_ref, scale_ref, out_ref, even_ref, odd_ref):
    bands, columns, lats = z_ref.shape
    per = lats // LANES
    half = bands * per // 2
    quarter = columns // FIELDS
    turn = (iota((LANES, LANES), 0) + iota((LANES, LANES), 1) == LANES - 1).astype(F32).astype(BF16)

    def place(i):
        return i // per, pl.ds((i % per) * LANES, LANES)

    for i in range(half):
        b, lanes = place(i)
        north = z_ref[b, :, lanes].astype(F32)
        b, lanes = place(2 * half - 1 - i)
        south = jnp.dot(z_ref[b, :, lanes], turn, preferred_element_type=F32)
        here = pl.ds(i * LANES, LANES)
        weight = rows_ref[1:2, here]
        even_ref[:, here] = ((north + south) * weight).astype(BF16)
        odd_ref[:, here] = ((north - south) * weight).astype(BF16)

    fresh = []
    for parity, side in ((0, even_ref), (1, odd_ref)):
        spec = lax.dot_general(side[...], table_ref[parity], (((1,), (1,)), ((), ())), preferred_element_type=F32)
        keep = degree_ref[parity, 0:1, :]
        weight = degree_ref[parity, 1:2, :]
        damp = degree_ref[parity, 2:3, :]
        middle = spec[quarter : 3 * quarter] * keep
        mixed = dot32(first_ref[...], middle)
        projected = (mixed[:quarter] + weight * mixed[quarter:]) / scale_ref[parity]
        after = dot32(second_ref[...], projected)
        fresh.append(
            jnp.concatenate(
                [
                    spec[:quarter] * damp,
                    after[:quarter],
                    middle[quarter:] - after[quarter:],
                    spec[3 * quarter :] * damp,
                ],
                axis=0,
            ).astype(BF16)
        )
    even = jnp.dot(fresh[0], table_ref[0], preferred_element_type=F32)
    odd = jnp.dot(fresh[1], table_ref[1], preferred_element_type=F32)
    for i in range(half):
        here = slice(i * LANES, (i + 1) * LANES)
        live = rows_ref[0:1, here]
        b, lanes = place(i)
        out_ref[b, :, lanes] = ((even[:, here] + odd[:, here]) * live).astype(BF16)
        lower = ((even[:, here] - odd[:, here]) * live).astype(BF16)
        b, lanes = place(2 * half - 1 - i)
        out_ref[b, :, lanes] = jnp.dot(lower, turn, preferred_element_type=F32).astype(BF16)


def whole(shape):
    return pl.BlockSpec(shape, lambda *_: (0,) * len(shape))


def permute(kernel, name, lookup, x, width):
    columns, lats = x.shape
    block = min(columns, 512)
    return pl.pallas_call(
        functools.partial(kernel, width, block),
        name=name,
        grid=(columns // block,),
        in_specs=[whole(lookup.shape), whole(x.shape)],
        out_specs=pl.BlockSpec((block, lats), lambda i: (i, 0)),
        out_shape=jax.ShapeDtypeStruct(x.shape, BF16),
        compiler_params=pltpu.CompilerParams(vmem_limit_bytes=VMEM_BYTES),
        cost_estimate=pl.CostEstimate(flops=2 * columns * columns * lats, bytes_accessed=4 * columns * lats, transcendentals=0),
    )(lookup, x)


def per_device(
    azimuthal_coeffs,
    polynomial_tables,
    gauss_masses,
    circle_samples,
    table_lookup,
    eigen_basis,
    basis_mapping,
    eigen_constants,
    hydrostatic_matrix,
    thermal_response,
):
    lats, levels, width = azimuthal_coeffs.shape
    waves = width // 2
    bands = lax.axis_size("band")
    levs = lax.axis_size("lev")
    devices = bands * levs
    columns = 2 * levels * levs
    table = polynomial_tables[0]
    nth, lath = table.shape[1:]
    lookup = table_lookup.reshape(1, waves)

    x = jnp.transpose(azimuthal_coeffs, (1, 2, 0)).reshape(levels * width, lats)
    sent = permute(send_kernel, "send", lookup, x, width).reshape(devices, 2 * levels, lats)
    got = lax.all_to_all(sent, ("band", "lev"), 0, 0, tiled=True).reshape(bands, columns, lats)

    n = 2 * eigen_basis.shape[0]
    small = [
        lookup,
        gauss_masses.reshape(1, lath),
        circle_samples.reshape(1, lath),
        eigen_basis,
        basis_mapping,
        eigen_constants.reshape(1, n // 2),
        hydrostatic_matrix,
        thermal_response,
    ]
    made = [(2, lath), (2 * n, 2 * n), (2 * n, n), (2, 3, nth), (2, n, nth)]
    prepared = pl.pallas_call(
        functools.partial(prep_kernel, levs),
        name="prep",
        out_shape=[jax.ShapeDtypeStruct(shape, F32) for shape in made],
        compiler_params=pltpu.CompilerParams(vmem_limit_bytes=VMEM_BYTES),
        cost_estimate=pl.CostEstimate(flops=10**8, bytes_accessed=10**6, transcendentals=0),
    )(*small)

    aligned = lats % LANES == 0 and bands % 2 == 0
    if not aligned:
        got = jnp.transpose(got.reshape(2, bands // 2, columns, lats), (0, 2, 1, 3)).reshape(2, columns, lath)
    result = pl.pallas_call(
        step_kernel,
        name="step",
        out_shape=jax.ShapeDtypeStruct(got.shape, BF16),
        scratch_shapes=[pltpu.VMEM((columns, lath), BF16)] * 2,
        compiler_params=pltpu.CompilerParams(vmem_limit_bytes=VMEM_BYTES),
        cost_estimate=pl.CostEstimate(
            flops=8 * columns * nth * lath, bytes_accessed=4 * nth * lath + 8 * columns * lath, transcendentals=0
        ),
    )(got, table, *prepared)
    if not aligned:
        result = jnp.transpose(result.reshape(2, columns, bands // 2, lats), (0, 2, 1, 3))
    result = result.reshape(devices, 2 * levels, lats)

    returned = lax.all_to_all(result, ("band", "lev"), 0, 0, tiled=True).reshape(levels * width, lats)
    out = permute(back_kernel, "back", lookup, returned, width)
    return jnp.transpose(out.reshape(levels, width, lats), (2, 0, 1))


def solution(mesh):
    placed = (P("band", "lev", None), P(("band", "lev"), None, None, None)) + (P(),) * 8
    return jax.shard_map(
        per_device, mesh=mesh, in_specs=placed, out_specs=P("band", "lev", None), check_vma=False
    )
```

time: 95.6 us -> 55.2 us (0.58)
  waiting for transfers between devices: 42.2 us -> 18.2 us
  local copies, waits for them, and re-layouts: 13.4 us -> 1.94 us
  blocking collectives: 12.6 us -> 21.2 us
  starting transfers between devices: 14.4 us -> 7.33 us
  matrix products: 6.71 us -> 0 us
  Pallas kernels: 0 us -> 6.23 us
  other arithmetic: 4.69 us -> 0 us
  between operations: 1.12 us -> 0.14 us
    all_to_all x3 -> x1, waiting for transfers between devices: 42.2 us -> 18.2 us  [per_device(): lax.all_to_all(sent, ('band', 'lev'), 0, 0, tiled=True)]
    all_to_all x1, blocking collectives: 12.6 us -> 21.2 us  [per_device(): lax.all_to_all(result, ('band', 'lev'), 0, 0, tiled=True)]
    all_to_all x3 -> x1, starting transfers between devices: 14.4 us -> 7.33 us  [per_device(): lax.all_to_all(sent, ('band', 'lev'), 0, 0, tiled=True)]
    dot_general x8 -> x0, matrix products: 6.71 us -> none  [the longest x1 1.99 us: analyse_wave(): jnp.dot(operator_array[0], even_part, preferred_element_type=jnp.float32)]
    pallas_call x0 -> x4, Pallas kernels: none -> 6.23 us  [the longest x2 3.05 us: permute(): pl.pallas_call(functools.partial(kernel, width, block), name=name, grid=(...]
    gather x2 -> x0, local copies, waits for them, and re-layouts: 3.21 us -> none  [the longest x1 2.54 us: per_device(): ordered = jnp.take(azimuthal_coeffs, column_pick, axis=2)]
    all_to_all x3 -> x0, local copies, waits for them, and re-layouts: 2.55 us -> none  [the longest x1 1.31 us: per_device(): lax.all_to_all(result[:, None, :], 'band', split_axis=0, concat_axis=1, t...]
    reshape x3 -> x2, local copies, waits for them, and re-layouts: 1.61 us -> 0.01 us  [the longest x1 0.01 us: per_device(): gauss_masses.reshape(1, lath)]
  transfers between devices with their start and end apart: 3 -> 1, of which waited for: 3 -> 1; matrix products, arithmetic and copies ran while one was open for 2% -> 0% of each run, Pallas kernels for 0% -> 1%
where the time goes in v1:
time: 55.2 us; the launch traced here: 55 us
  blocking collectives  21.2 us (38%)
  waiting for transfers between devices  18.2 us (33%)
  starting transfers between devices  7.33 us (13%)
  Pallas kernels  6.23 us (11%)
  local copies, waits for them, and re-layouts  1.94 us (4%)
    all_to_all x1, blocking collectives, per_device(): lax.all_to_all(result, ('band', 'lev'), 0, 0, tiled=True)  21.2 us
    all_to_all x1, waiting for transfers between devices, per_device(): lax.all_to_all(sent, ('band', 'lev'), 0, 0, tiled=True)  18.2 us
    all_to_all x1, starting transfers between devices, per_device(): lax.all_to_all(sent, ('band', 'lev'), 0, 0, tiled=True)  7.33 us
    pallas_call x2, Pallas kernels, permute(): pl.pallas_call(functools.partial(kernel, width, block), name=name, grid=(...  3.05 us
    pallas_call x1, Pallas kernels, per_device(): pl.pallas_call(step_kernel, name='step', out_shape=jax.ShapeDtypeStruct(g...  2.4 us
    unnamed x22, local copies, waits for them, and re-layouts  1.93 us
  transfers between devices with their start and end apart: 1, of which 1 were waited for; matrix products, arithmetic and copies ran while one was open for 0% of the time, Pallas kernels for 1%

profile of v1, /device:TPU:0, one launch (start us, length us, event | category | flops | bytes accessed | tf_op | source)
XLA Modules:
  0.0 55.0 jit_solution(4091897926467578179)
XLA Ops:
  0.0 0.0 copy-start
  0.0 0.0 copy-start.1
  0.0 1.2 %copy-done.1 = bf16[640,8,64]{0,2,1:T(8,128)(2,1)S(1)} copy-done((bf16[640,8,64]{0,2,1:T(8,128)(2,1)S(1)}, bf16[640,8,64]{0,2,1:T(8,128)(2,1)}, u32[]{:S(2)}) %copy-start.1) | copy-done | bytes 655384
  1.2 0.0 copy-start.2
  1.2 0.7 %copy-done.2 = s32[32]{0:T(128)S(1)} copy-done((s32[32]{0:T(128)S(1)}, s32[32]{0:T(128)}, u32[]{:S(2)}) %copy-start.2) | copy-done | bytes 152
  1.9 0.0 copy-start.9
  1.9 0.0 copy-start.10
  1.9 0.0 copy-start.3
  1.9 0.0 copy-start.4
  1.9 0.0 copy-start.5
  1.9 0.0 copy-start.6
  1.9 0.0 copy-start.7
  1.9 0.0 copy-start.8
  1.9 1.5 %send.1 = bf16[512,640]{1,0:T(8,128)(2,1)} custom-call(s32[1,32]{1,0:T(1,128)S(1)} %bitcast.18, bf16[512,640]{1,0:T(8,128)(2,1)S(1)} %bitcast.17), custom_call_target="tpu_custom_call" | custom-call | flops 335544320 | bytes 1310720 | tf_op jit(solution)/shard_map/send/pallas_call | solution.py:176
  3.5 7.3 %all-to-all-start = ((bf16[32,16,640]{2,1,0:T(8,128)(2,1)}), bf16[32,16,640]{2,1,0:T(8,128)(2,1)S(1)}, u32[]{:S(2)}, u32[]{:S(2)}) async-start(bf16[32,16,640]{2,1,0:T(8,128)(2,1)} %bitcast.3), calls=%async_computation | async-start | bytes 1310720 | tf_op jit(solution)/shard_map/all_to_all | solution.py:212
  10.8 0.0 copy-done.9
  10.9 0.0 copy-done.10
  10.9 0.0 copy-done.3
  10.9 0.0 copy-done.4
  10.9 0.0 copy-done.5
  10.9 0.0 copy-done.6
  10.9 0.0 copy-done.7
  10.9 0.0 copy-done.8
  10.9 0.8 %prep.1 = (f32[2,1280]{1,0:T(2,128)S(1)}, f32[64,64]{1,0:T(8,128)S(1)}, f32[64,32]{1,0:T(8,128)S(1)}, f32[2,3,448]{2,1,0:T(4,128)S(1)}, f32[2,32,448]{2,1,0:T(8,128)S(1)}) custom-call(s32[1,32]{1,0:T(1,128)S(1)} %bitcast.19, f32[1,1280]{1,0:T(1,128)S(1)} %reshape.34.masses_ref, s32[1,1280]{1,0:T(1,128)S(1)} %reshape.35.samples_ref, f32[16,16]{1,0:T(8,128)S(1)} %copy-done.4, ...), custom_call_target="tpu_custom_call" | custom-call | flops 100000000 | bytes 1000000 | tf_op jit(solution)/shard_map/prep/pallas_call | solution.py:226
  11.7 18.2 %all-to-all-done = bf16[32,16,640]{2,1,0:T(8,128)(2,1)S(1)} async-done(((bf16[32,16,640]{2,1,0:T(8,128)(2,1)}), bf16[32,16,640]{2,1,0:T(8,128)(2,1)S(1)}, u32[]{:S(2)}, u32[]{:S(2)}) %all-to-all-start) | async-done | bytes 655392 | tf_op jit(solution)/shard_map/all_to_all | solution.py:212
  29.9 0.0 copy-done
  29.9 2.4 %step.1 = bf16[4,128,640]{2,1,0:T(8,128)(2,1)S(1)} custom-call(bf16[4,128,640]{2,1,0:T(8,128)(2,1)S(1)} %bitcast.13, bf16[2,448,1280]{2,1,0:T(8,128)(2,1)S(1)} %bitcast.16, f32[2,1280]{1,0:T(2,128)S(1)} %get-tuple-element.10.rows_ref, f32[64,64]{1,0:T(8,128)S(1)} %get-tuple-element.11.first_ref, f32[64,32]{1,0:T(8,128)S(1)} %get-tuple-element.12.second_ref, ...), custom_call_target="tpu_custom_call" | custom-call | flops 587202560 | bytes 3604480 | tf_op jit(solution)/shard_map/step/pallas_call | solution.py:237
  32.3 21.2 %all_to_all.10 = bf16[32,16,640]{2,1,0:T(8,128)(2,1)S(1)} all-to-all(bf16[32,16,640]{2,1,0:T(8,128)(2,1)S(1)} %bitcast.14), channel_id=1, replica_groups=mesh['band'=4,'lev'=8] {'band','lev'}, dimensions={0} | all-to-all | bytes 1310720 | tf_op jit(solution)/shard_map/all_to_all | solution.py:251
  53.5 1.5 %back.1 = bf16[512,640]{1,0:T(8,128)(2,1)} custom-call(s32[1,32]{1,0:T(1,128)S(1)} %bitcast.20, bf16[512,640]{1,0:T(8,128)(2,1)S(1)} %bitcast.15), custom_call_target="tpu_custom_call" | custom-call | flops 335544320 | bytes 1310720 | tf_op jit(solution)/shard_map/back/pallas_call | solution.py:176
  (2 shorter events, 0.0 us)
Async XLA Ops:
  0.0 29.9 %copy-start = (bf16[1,2,448,1280]{3,2,1,0:T(8,128)(2,1)S(1)}, bf16[1,2,448,1280]{3,2,1,0:T(8,128)(2,1)}, u32[]{:S(2)}) copy-start(bf16[1,2,448,1280]{3,2,1,0:T(8,128)(2,1)} %param.11) | copy-start | bytes 6881284
  0.0 1.2 %copy-start.1 = (bf16[640,8,64]{0,2,1:T(8,128)(2,1)S(1)}, bf16[640,8,64]{0,2,1:T(8,128)(2,1)}, u32[]{:S(2)}) copy-start(bf16[640,8,64]{0,2,1:T(8,128)(2,1)} %param.10) | copy-start | bytes 1966084
  1.2 0.7 %copy-start.2 = (s32[32]{0:T(128)S(1)}, s32[32]{0:T(128)}, u32[]{:S(2)}) copy-start(s32[32]{0:T(128)} %param.14) | copy-start | bytes 388
  1.9 8.9 %copy-start.9 = (f32[1280]{0:T(1024)S(1)}, f32[1280]{0:T(1024)}, u32[]{:S(2)}) copy-start(f32[1280]{0:T(1024)} %param.12) | copy-start | bytes 15364
  1.9 9.0 %copy-start.10 = (s32[1280]{0:T(1024)S(1)}, s32[1280]{0:T(1024)}, u32[]{:S(2)}) copy-start(s32[1280]{0:T(1024)} %param.13) | copy-start | bytes 15364
  1.9 9.0 %copy-start.3 = (s32[32]{0:T(128)S(1)}, s32[32]{0:T(128)}, u32[]{:S(2)}) copy-start(s32[32]{0:T(128)} %param.14) | copy-start | bytes 388
  1.9 9.0 %copy-start.4 = (f32[16,16]{1,0:T(8,128)S(1)}, f32[16,16]{1,0:T(8,128)}, u32[]{:S(2)}) copy-start(f32[16,16]{1,0:T(8,128)} %eigen_basis_ref.1) | copy-start | bytes 3076
  1.9 9.0 %copy-start.5 = (f32[16,16]{1,0:T(8,128)S(1)}, f32[16,16]{1,0:T(8,128)}, u32[]{:S(2)}) copy-start(f32[16,16]{1,0:T(8,128)} %basis_mapping_ref.1) | copy-start | bytes 3076
  1.9 9.0 %copy-start.6 = (f32[16,16]{1,0:T(8,128)S(1)}, f32[16,16]{1,0:T(8,128)}, u32[]{:S(2)}) copy-start(f32[16,16]{1,0:T(8,128)} %hydrostatic_ref.1) | copy-start | bytes 3076
  1.9 9.0 %copy-start.7 = (f32[16,16]{1,0:T(8,128)S(1)}, f32[16,16]{1,0:T(8,128)}, u32[]{:S(2)}) copy-start(f32[16,16]{1,0:T(8,128)} %thermal_ref.1) | copy-start | bytes 3076
  1.9 9.0 %copy-start.8 = (f32[16]{0:T(128)S(1)}, f32[16]{0:T(128)}, u32[]{:S(2)}) copy-start(f32[16]{0:T(128)} %param.17) | copy-start | bytes 196
  3.5 26.4 %all-to-all-start = ((bf16[32,16,640]{2,1,0:T(8,128)(2,1)}), bf16[32,16,640]{2,1,0:T(8,128)(2,1)S(1)}, u32[]{:S(2)}, u32[]{:S(2)}) async-start(bf16[32,16,640]{2,1,0:T(8,128)(2,1)} %bitcast.3), calls=%async_computation | async-start | bytes 1310720 | tf_op jit(solution)/shard_map/all_to_all | solution.py:212

commit v2 on v1

v2 whole, which is shorter than its diff:
```python
import functools

import jax
import jax.numpy as jnp
from jax import lax
from jax.experimental import pallas as pl
from jax.experimental.pallas import tpu as pltpu
from jax.sharding import PartitionSpec as P

TRUNC = 1280
FIELDS = 4
STIFFNESS = 8.0
DIFFUSION = 4.0
LANES = 128
SUBLANES = 8
HIGHEST = lax.Precision.HIGHEST
F32 = jnp.float32
BF16 = jnp.bfloat16
I32 = jnp.int32
VMEM_BYTES = 24 * 2**20


def iota(shape, dim):
    return lax.broadcasted_iota(I32, shape, dim)


def dot32(a, b):
    return jnp.dot(a, b, precision=HIGHEST, preferred_element_type=F32)


def halves(x):
    high = x.astype(BF16)
    return high, (x - high.astype(F32)).astype(BF16)


def send_kernel(width, lookup_hbm, x_hbm, out_ref, lookup, held, wide, small_sem, sems):
    columns, lats = x_hbm.shape
    levels, waves, tiles = columns // width, width // 2, lats // LANES
    copies = [
        pltpu.make_async_copy(x_hbm.at[:, pl.ds(t * LANES, LANES)], held.at[t], sems.at[t]) for t in range(tiles)
    ]
    small = pltpu.make_async_copy(lookup_hbm, lookup, small_sem)
    small.start()
    for copy in copies:
        copy.start()
    small.wait()
    for t in range(tiles):
        copies[t].wait()
        wide[t] = held[t].astype(F32)
        for m in range(waves):
            parts = [wide[t, pl.ds(2 * m + c, levels, stride=width), :] for c in range(2)]
            out_ref[lookup[m], :, pl.ds(t * LANES, LANES)] = jnp.concatenate(parts, axis=0).astype(BF16)


def back_kernel(width, lookup_hbm, x_ref, out_hbm, lookup, held, wide, small_sem, sems):
    columns, lats = out_hbm.shape
    levels, waves, tiles = columns // width, width // 2, lats // LANES
    small = pltpu.make_async_copy(lookup_hbm, lookup, small_sem)
    small.start()
    small.wait()
    copies = []
    for t in range(tiles):
        for m in range(waves):
            block = x_ref[lookup[m], :, pl.ds(t * LANES, LANES)].astype(F32)
            for c in range(2):
                wide[t, pl.ds(2 * m + c, levels, stride=width), :] = block[c * levels : (c + 1) * levels]
        held[t] = wide[t].astype(BF16)
        copy = pltpu.make_async_copy(held.at[t], out_hbm.at[:, pl.ds(t * LANES, LANES)], sems.at[t])
        copy.start()
        copies.append(copy)
    for copy in copies:
        copy.wait()


def owner_rows(lookup, width, columns):
    waves = lookup.shape[1]
    levels = columns // width
    row = iota((1, columns), 1)
    pick = (iota((waves, columns), 0) == lax.div(lax.rem(iota((waves, columns), 1), width), 2)).astype(F32)
    owner = dot32(lookup.astype(F32), pick).astype(I32)
    return owner * (2 * levels) + lax.rem(row, 2) * levels + lax.div(row, width)


def send_by_matmul(width, block, lookup_ref, x_ref, out_ref):
    columns = x_ref.shape[0]
    target = owner_rows(lookup_ref[...], width, columns)
    row = iota((block, columns), 0) + pl.program_id(0) * block
    pick = (row == target).astype(F32).astype(BF16)
    out_ref[...] = jnp.dot(pick, x_ref[...], preferred_element_type=F32).astype(BF16)


def back_by_matmul(width, block, lookup_ref, x_ref, out_ref):
    columns = x_ref.shape[0]
    waves = lookup_ref.shape[1]
    levels = columns // width
    row = iota((block, 1), 0) + pl.program_id(0) * block
    mine = iota((block, waves), 1) == lax.div(lax.rem(iota((block, waves), 0) + pl.program_id(0) * block, width), 2)
    owner = jnp.sum(jnp.where(mine, lookup_ref[...].astype(F32), 0.0), axis=1, keepdims=True).astype(I32)
    target = owner * (2 * levels) + lax.rem(row, 2) * levels + lax.div(row, width)
    pick = (iota((block, columns), 1) == target).astype(F32).astype(BF16)
    out_ref[...] = jnp.dot(pick, x_ref[...], preferred_element_type=F32).astype(BF16)


def level_of(row, levels):
    return lax.div(row, 2 * levels) * levels + lax.rem(row, levels)


def part_of(row, levels):
    return lax.rem(lax.div(row, levels), 2)


def pair_up(small, levels):
    n = small.shape[0]
    left = (level_of(iota((2 * n, n), 0), levels) == iota((2 * n, n), 1)).astype(F32)
    right = (iota((n, 2 * n), 0) == level_of(iota((n, 2 * n), 1), levels)).astype(F32)
    square = (2 * n, 2 * n)
    same = part_of(iota(square, 0), levels) == part_of(iota(square, 1), levels)
    return jnp.where(same, dot32(dot32(left, small), right), 0.0)


def mix(matrix, values):
    high, low = halves(matrix)
    top, rest = halves(values)
    return jnp.dot(
        jnp.concatenate([high, high, low], axis=1),
        jnp.concatenate([top, rest, top], axis=0),
        preferred_element_type=F32,
    )


def step_kernel(
    lev_count,
    levels,
    z_ref,
    table_ref,
    lookup_ref,
    masses_ref,
    samples_ref,
    eigen_basis_ref,
    basis_mapping_ref,
    eigen_constants_ref,
    hydrostatic_ref,
    thermal_ref,
    out_ref,
    even_ref,
    odd_ref,
):
    bands, columns, lats = z_ref.shape
    per = lats // LANES
    half = bands * per // 2
    quarter = columns // FIELDS
    nth = table_ref.shape[1]
    turn = (iota((LANES, LANES), 0) + iota((LANES, LANES), 1) == LANES - 1).astype(F32).astype(BF16)

    waves = lookup_ref.shape[1]
    me = lax.axis_index("band") * lev_count + lax.axis_index("lev")
    wave = jnp.sum(
        jnp.where(lookup_ref[...] == me, iota((1, waves), 1), 0).astype(F32), axis=1, keepdims=True
    ).astype(I32)
    live = (2 * wave < samples_ref[...]).astype(F32)
    weights = masses_ref[...] * live

    def place(i):
        return i // per, pl.ds((i % per) * LANES, LANES)

    for i in range(half):
        b, lanes = place(i)
        north = z_ref[b, :, lanes].astype(F32)
        b, lanes = place(2 * half - 1 - i)
        south = jnp.dot(z_ref[b, :, lanes], turn, preferred_element_type=F32)
        here = slice(i * LANES, (i + 1) * LANES)
        weight = weights[:, here]
        even_ref[:, here] = ((north + south) * weight).astype(BF16)
        odd_ref[:, here] = ((north - south) * weight).astype(BF16)

    mapping = pair_up(basis_mapping_ref[...], levels)
    basis = pair_up(eigen_basis_ref[...], levels)
    from_heat = dot32(mapping, pair_up(hydrostatic_ref[...], levels))
    to_heat = dot32(pair_up(thermal_ref[...], levels), basis)
    nothing = jnp.zeros((quarter, quarter), F32)
    first = jnp.concatenate(
        [jnp.concatenate([mapping, nothing], axis=1), jnp.concatenate([nothing, from_heat], axis=1)], axis=0
    )
    second = jnp.concatenate([basis, to_heat], axis=0)
    spread = (quarter, quarter // 2)
    chosen = level_of(iota(spread, 0), levels) == iota(spread, 1)
    constants = jnp.sum(jnp.where(chosen, eigen_constants_ref[...], 0.0), axis=1, keepdims=True)

    fresh = []
    for parity, side in ((0, even_ref), (1, odd_ref)):
        spec = lax.dot_general(side[...], table_ref[parity], (((1,), (1,)), ((), ())), preferred_element_type=F32)
        degree = iota((1, nth), 1) * 2 + wave + parity
        keep = (degree < TRUNC).astype(F32)
        order = degree.astype(F32)
        scaled = order * (order + 1.0) / (TRUNC * (TRUNC + 1.0))
        weight = STIFFNESS * scaled
        damp = keep / (1.0 + DIFFUSION * scaled * scaled)
        middle = spec[quarter : 3 * quarter] * keep
        mixed = mix(first, middle)
        projected = (mixed[:quarter] + weight * mixed[quarter:]) / (1.0 + weight * constants)
        after = mix(second, projected)
        fresh.append(
            jnp.concatenate(
                [
                    spec[:quarter] * damp,
                    after[:quarter],
                    middle[quarter:] - after[quarter:],
                    spec[3 * quarter :] * damp,
                ],
                axis=0,
            ).astype(BF16)
        )
    even = jnp.dot(fresh[0], table_ref[0], preferred_element_type=F32)
    odd = jnp.dot(fresh[1], table_ref[1], preferred_element_type=F32)
    for i in range(half):
        here = slice(i * LANES, (i + 1) * LANES)
        b, lanes = place(i)
        out_ref[b, :, lanes] = ((even[:, here] + odd[:, here]) * live[:, here]).astype(BF16)
        lower = ((even[:, here] - odd[:, here]) * live[:, here]).astype(BF16)
        b, lanes = place(2 * half - 1 - i)
        out_ref[b, :, lanes] = jnp.dot(lower, turn, preferred_element_type=F32).astype(BF16)


def whole(shape):
    return pl.BlockSpec(shape, lambda *_: (0,) * len(shape))


def by_matmul(kernel, name, lookup, x, width):
    columns, lats = x.shape
    block = min(columns, 512)
    return pl.pallas_call(
        functools.partial(kernel, width, block),
        name=name,
        grid=(columns // block,),
        in_specs=[whole(lookup.shape), whole(x.shape)],
        out_specs=pl.BlockSpec((block, lats), lambda i: (i, 0)),
        out_shape=jax.ShapeDtypeStruct(x.shape, BF16),
        compiler_params=pltpu.CompilerParams(vmem_limit_bytes=VMEM_BYTES),
    )(lookup, x)


ANY = pl.BlockSpec(memory_space=pl.ANY)
VMEM = pl.BlockSpec(memory_space=pltpu.VMEM)


def by_rows(kernel, name, lookup, x, out_shape, columns, width, lats, in_spec, out_spec):
    tiles = lats // LANES
    return pl.pallas_call(
        functools.partial(kernel, width),
        name=name,
        in_specs=[ANY, in_spec],
        out_specs=out_spec,
        out_shape=jax.ShapeDtypeStruct(out_shape, BF16),
        scratch_shapes=[
            pltpu.SMEM(lookup.shape, I32),
            pltpu.VMEM((tiles, columns, LANES), BF16),
            pltpu.VMEM((tiles, columns, LANES), F32),
            pltpu.SemaphoreType.DMA,
            pltpu.SemaphoreType.DMA((tiles,)),
        ],
        compiler_params=pltpu.CompilerParams(vmem_limit_bytes=VMEM_BYTES),
    )(lookup, x)


def per_device(
    azimuthal_coeffs,
    polynomial_tables,
    gauss_masses,
    circle_samples,
    table_lookup,
    eigen_basis,
    basis_mapping,
    eigen_constants,
    hydrostatic_matrix,
    thermal_response,
):
    lats, levels, width = azimuthal_coeffs.shape
    waves = width // 2
    bands = lax.axis_size("band")
    levs = lax.axis_size("lev")
    devices = bands * levs
    columns = 2 * levels * levs
    local = levels * width
    table = polynomial_tables[0]
    nth, lath = table.shape[1:]
    lookup = table_lookup.reshape(1, waves)
    aligned = lats % LANES == 0 and bands % 2 == 0
    strided = aligned and levels == SUBLANES and waves <= 64

    x = jnp.transpose(azimuthal_coeffs, (1, 2, 0)).reshape(local, lats)
    blocks = (devices, 2 * levels, lats)
    if strided:
        sent = by_rows(send_kernel, "send", table_lookup, x, blocks, local, width, lats, ANY, VMEM)
    else:
        sent = by_matmul(send_by_matmul, "send", lookup, x, width).reshape(blocks)
    got = lax.all_to_all(sent, ("band", "lev"), 0, 0, tiled=True).reshape(bands, columns, lats)

    if not aligned:
        got = jnp.transpose(got.reshape(2, bands // 2, columns, lats), (0, 2, 1, 3)).reshape(2, columns, lath)
    result = pl.pallas_call(
        functools.partial(step_kernel, levs, levels),
        name="step",
        out_shape=jax.ShapeDtypeStruct(got.shape, BF16),
        scratch_shapes=[pltpu.VMEM((columns, lath), BF16)] * 2,
        compiler_params=pltpu.CompilerParams(vmem_limit_bytes=VMEM_BYTES),
        cost_estimate=pl.CostEstimate(
            flops=8 * columns * nth * lath, bytes_accessed=4 * nth * lath + 8 * columns * lath, transcendentals=0
        ),
    )(
        got,
        table,
        lookup,
        gauss_masses.reshape(1, lath),
        circle_samples.reshape(1, lath),
        eigen_basis,
        basis_mapping,
        eigen_constants.reshape(1, eigen_constants.shape[0]),
        hydrostatic_matrix,
        thermal_response,
    )
    if not aligned:
        result = jnp.transpose(result.reshape(2, columns, bands // 2, lats), (0, 2, 1, 3))

    returned = lax.all_to_all(result.reshape(blocks), ("band", "lev"), 0, 0, tiled=True)
    if strided:
        out = by_rows(back_kernel, "back", table_lookup, returned, (local, lats), local, width, lats, VMEM, ANY)
    else:
        out = by_matmul(back_by_matmul, "back", lookup, returned.reshape(local, lats), width)
    return jnp.transpose(out.reshape(levels, width, lats), (2, 0, 1))


def solution(mesh):
    placed = (P("band", "lev", None), P(("band", "lev"), None, None, None)) + (P(),) * 8
    return jax.shard_map(
        per_device, mesh=mesh, in_specs=placed, out_specs=P("band", "lev", None), check_vma=False
    )
```

time: 55.2 us -> 57 us (1.033)
  Pallas kernels: 6.23 us -> 7.16 us
  waiting for transfers between devices: 18.2 us -> 19 us
    pallas_call x4 -> x3, Pallas kernels: 6.23 us -> 7.16 us  [the longest x2 4.47 us: by_rows(): pl.pallas_call(functools.partial(kernel, width), name=name, in_specs=[ANY...]
    all_to_all x1, waiting for transfers between devices: 18.2 us -> 19 us  [per_device(): lax.all_to_all(sent, ('band', 'lev'), 0, 0, tiled=True)]
  transfers between devices with their start and end apart: 1 -> 1, of which waited for: 1 -> 1; matrix products, arithmetic and copies ran while one was open for 0% -> 0% of each run, Pallas kernels for 1% -> 0%
where the time goes in v2:
time: 57 us; the launch traced here: 56.8 us
  blocking collectives  21.2 us (37%)
  waiting for transfers between devices  19 us (33%)
  starting transfers between devices  7.33 us (13%)
  Pallas kernels  7.16 us (13%)
  local copies, waits for them, and re-layouts  1.94 us (3%)
    all_to_all x1, blocking collectives, per_device(): lax.all_to_all(result.reshape(blocks), ('band', 'lev'), 0, 0, tiled=True)  21.2 us
    all_to_all x1, waiting for transfers between devices, per_device(): lax.all_to_all(sent, ('band', 'lev'), 0, 0, tiled=True)  19 us
    all_to_all x1, starting transfers between devices, per_device(): lax.all_to_all(sent, ('band', 'lev'), 0, 0, tiled=True)  7.33 us
    pallas_call x2, Pallas kernels, by_rows(): pl.pallas_call(functools.partial(kernel, width), name=name, in_specs=[ANY...  4.47 us
    pallas_call x1, Pallas kernels, per_device(): pl.pallas_call(functools.partial(step_kernel, levs, levels), name='step',...  2.7 us
    unnamed x22, local copies, waits for them, and re-layouts  1.93 us
  transfers between devices with their start and end apart: 1, of which 1 were waited for; matrix products, arithmetic and copies ran while one was open for 0% of the time, Pallas kernels for 0%

profile of v2, /device:TPU:0, one launch (start us, length us, event | category | flops | bytes accessed | tf_op | source)
XLA Modules:
  0.0 56.8 jit_solution(16414966120452485969)
XLA Ops:
  0.0 0.0 copy-start
  0.0 0.0 copy-start.1
  0.0 1.2 %copy-done.1 = bf16[640,8,64]{0,2,1:T(8,128)(2,1)S(1)} copy-done((bf16[640,8,64]{0,2,1:T(8,128)(2,1)S(1)}, bf16[640,8,64]{0,2,1:T(8,128)(2,1)}, u32[]{:S(2)}) %copy-start.1) | copy-done | bytes 655384
  1.2 0.0 copy-start.6
  1.2 0.7 %copy-done.6 = s32[32]{0:T(128)S(1)} copy-done((s32[32]{0:T(128)S(1)}, s32[32]{0:T(128)}, u32[]{:S(2)}) %copy-start.6) | copy-done | bytes 152
  1.9 0.0 copy-start.9
  1.9 0.0 copy-start.10
  1.9 0.0 copy-start.2
  1.9 0.0 copy-start.3
  1.9 0.0 copy-start.4
  1.9 0.0 copy-start.5
  1.9 0.0 copy-start.7
  1.9 0.0 copy-start.8
  1.9 2.3 %send.1 = bf16[32,16,640]{2,1,0:T(8,128)(2,1)} custom-call(s32[32]{0:T(128)S(1)} %copy-done.6, bf16[512,640]{1,0:T(8,128)(2,1)S(1)} %bitcast.14), custom_call_target="tpu_custom_call" | custom-call | tf_op jit(solution)/shard_map/send/pallas_call | solution.py:248
  4.3 7.3 %all-to-all-start = ((bf16[32,16,640]{2,1,0:T(8,128)(2,1)}), bf16[32,16,640]{2,1,0:T(8,128)(2,1)S(1)}, u32[]{:S(2)}, u32[]{:S(2)}) async-start(bf16[32,16,640]{2,1,0:T(8,128)(2,1)} %send.1), calls=%async_computation | async-start | bytes 1310720 | tf_op jit(solution)/shard_map/all_to_all | solution.py:296
  11.6 0.0 copy-done.9
  11.6 0.0 copy-done.10
  11.6 19.0 %all-to-all-done = bf16[32,16,640]{2,1,0:T(8,128)(2,1)S(1)} async-done(((bf16[32,16,640]{2,1,0:T(8,128)(2,1)}), bf16[32,16,640]{2,1,0:T(8,128)(2,1)S(1)}, u32[]{:S(2)}, u32[]{:S(2)}) %all-to-all-start) | async-done | bytes 655392 | tf_op jit(solution)/shard_map/all_to_all | solution.py:296
  30.6 0.0 copy-done
  30.6 0.0 copy-done.2
  30.6 0.0 copy-done.3
  30.7 0.0 copy-done.4
  30.7 0.0 copy-done.5
  30.7 0.0 copy-done.7
  30.7 0.0 copy-done.8
  30.7 2.7 %step.1 = bf16[4,128,640]{2,1,0:T(8,128)(2,1)S(1)} custom-call(bf16[4,128,640]{2,1,0:T(8,128)(2,1)S(1)} %bitcast.11, bf16[2,448,1280]{2,1,0:T(8,128)(2,1)S(1)} %bitcast.13, s32[1,32]{1,0:T(1,128)S(1)} %bitcast.15, f32[1,1280]{1,0:T(1,128)S(1)} %reshape.27.masses_ref, s32[1,1280]{1,0:T(1,128)S(1)} %reshape.28.samples_ref, f32[16,16]{1,0:T(8,128)S(1)} %copy-done.2, ...), custom_call_target="tpu_custom_call" | custom-call | flops 587202560 | bytes 3604480 | tf_op jit(solution)/shard_map/step/pallas_call | solution.py:300
  33.4 21.2 %all_to_all.10.x_ref = bf16[32,16,640]{2,1,0:T(8,128)(2,1)S(1)} all-to-all(bf16[32,16,640]{2,1,0:T(8,128)(2,1)S(1)} %bitcast.12), channel_id=1, replica_groups=mesh['band'=4,'lev'=8] {'band','lev'}, dimensions={0} | all-to-all | bytes 1310720 | tf_op jit(solution)/shard_map/all_to_all | solution.py:324
  54.6 2.2 %back.1 = bf16[512,640]{1,0:T(8,128)(2,1)} custom-call(s32[32]{0:T(128)S(1)} %copy-done.7, bf16[32,16,640]{2,1,0:T(8,128)(2,1)S(1)} %all_to_all.10.x_ref), custom_call_target="tpu_custom_call" | custom-call | tf_op jit(solution)/shard_map/back/pallas_call | solution.py:248
  (2 shorter events, 0.0 us)
Async XLA Ops:
  0.0 30.6 %copy-start = (bf16[1,2,448,1280]{3,2,1,0:T(8,128)(2,1)S(1)}, bf16[1,2,448,1280]{3,2,1,0:T(8,128)(2,1)}, u32[]{:S(2)}) copy-start(bf16[1,2,448,1280]{3,2,1,0:T(8,128)(2,1)} %param.11) | copy-start | bytes 6881284
  0.0 1.2 %copy-start.1 = (bf16[640,8,64]{0,2,1:T(8,128)(2,1)S(1)}, bf16[640,8,64]{0,2,1:T(8,128)(2,1)}, u32[]{:S(2)}) copy-start(bf16[640,8,64]{0,2,1:T(8,128)(2,1)} %param.10) | copy-start | bytes 1966084
  1.2 0.7 %copy-start.6 = (s32[32]{0:T(128)S(1)}, s32[32]{0:T(128)}, u32[]{:S(2)}) copy-start(s32[32]{0:T(128)} %lookup_hbm.3) | copy-start | bytes 388
  1.9 9.7 %copy-start.9 = (f32[1280]{0:T(1024)S(1)}, f32[1280]{0:T(1024)}, u32[]{:S(2)}) copy-start(f32[1280]{0:T(1024)} %param.12) | copy-start | bytes 15364
  1.9 9.7 %copy-start.10 = (s32[1280]{0:T(1024)S(1)}, s32[1280]{0:T(1024)}, u32[]{:S(2)}) copy-start(s32[1280]{0:T(1024)} %param.13) | copy-start | bytes 15364
  1.9 28.7 %copy-start.2 = (f32[16,16]{1,0:T(8,128)S(1)}, f32[16,16]{1,0:T(8,128)}, u32[]{:S(2)}) copy-start(f32[16,16]{1,0:T(8,128)} %eigen_basis_ref.1) | copy-start | bytes 3076
  1.9 28.7 %copy-start.3 = (f32[16,16]{1,0:T(8,128)S(1)}, f32[16,16]{1,0:T(8,128)}, u32[]{:S(2)}) copy-start(f32[16,16]{1,0:T(8,128)} %basis_mapping_ref.1) | copy-start | bytes 3076
  1.9 28.7 %copy-start.4 = (f32[16,16]{1,0:T(8,128)S(1)}, f32[16,16]{1,0:T(8,128)}, u32[]{:S(2)}) copy-start(f32[16,16]{1,0:T(8,128)} %hydrostatic_ref.1) | copy-start | bytes 3076
  1.9 28.7 %copy-start.5 = (f32[16,16]{1,0:T(8,128)S(1)}, f32[16,16]{1,0:T(8,128)}, u32[]{:S(2)}) copy-start(f32[16,16]{1,0:T(8,128)} %thermal_ref.1) | copy-start | bytes 3076
  1.9 28.7 %copy-start.7 = (s32[32]{0:T(128)S(1)}, s32[32]{0:T(128)}, u32[]{:S(2)}) copy-start(s32[32]{0:T(128)} %lookup_hbm.3) | copy-start | bytes 388
  1.9 28.7 %copy-start.8 = (f32[16]{0:T(128)S(1)}, f32[16]{0:T(128)}, u32[]{:S(2)}) copy-start(f32[16]{0:T(128)} %param.17) | copy-start | bytes 196
  4.3 26.4 %all-to-all-start = ((bf16[32,16,640]{2,1,0:T(8,128)(2,1)}), bf16[32,16,640]{2,1,0:T(8,128)(2,1)S(1)}, u32[]{:S(2)}, u32[]{:S(2)}) async-start(bf16[32,16,640]{2,1,0:T(8,128)(2,1)} %send.1), calls=%async_computation | async-start | bytes 1310720 | tf_op jit(solution)/shard_map/all_to_all | solution.py:296
